TPU v7x, 32 devices: a whole 2x2x4 slice. The times are simulated.
32 devices in a mesh: groups: 2 (over x), seq: 16 (over z, y, core).
Axes of the slice: x: 2, y: 2, z: 4, core: 2. Of those that a mesh axis runs over, the one named last changes fastest.
Arguments:
- queries: bfloat16 [4096, 2048], P(('groups', 'seq')), parts along dimension 0, may hold values from -8 to 8
- key_input: bfloat16 [4096, 2048], P(('groups', 'seq')), parts along dimension 0, may hold values from -4.5 to 4.5
- value_input: bfloat16 [4096, 2048], P(('groups', 'seq')), parts along dimension 0, may hold values from -6 to 6
- cotangent: bfloat16 [4096, 2048], P(('groups', 'seq')), parts along dimension 0, may hold values from -6 to 6
Outputs:
- attended: bfloat16 [4096, 2048], P(('groups', 'seq')), parts along dimension 0
- grad_queries: bfloat16 [4096, 2048], P(('groups', 'seq')), parts along dimension 0
- grad_keys: bfloat16 [4096, 2048], P(('groups', 'seq')), parts along dimension 0
- grad_values: bfloat16 [4096, 2048], P(('groups', 'seq')), parts along dimension 0
There are 2 independent parts, one for each index of `groups`. A program takes and returns all parts, laid end to end along the dimension named above; each array names one. Nothing has to cross between parts.
All inputs are finite; a program needn't handle non-finite values.
Results may differ from a plain program's by a relative error of at most 0.024.
Values may be sent and summed in bfloat16 or wider, within the bound.
A program may use at most 128 MiB of HBM per device.

v0:
```python
import functools
import math

import jax
import jax.numpy as jnp
from jax import lax
from jax.sharding import PartitionSpec as P

HEADS = 16
HEAD_DIM = 128
BLOCK = 64
LEVELS = 3


log_two = math.log(2.0)
masked_score = -1e30


def shifted(value, axis, steps):
    count = lax.axis_size(axis)
    initial, last = (max(0, -steps), min(count, count - steps))
    return lax.ppermute(value, axis, [(source, source + steps) for source in range(initial, last)])


def with_halo(cells, sides, width):
    for axis, dim in sides:
        count = lax.axis_size(axis)
        ends = count - 1
        head = lax.slice_in_dim(cells, 0, width, axis=dim)
        tail = lax.slice_in_dim(cells, cells.shape[dim] - width, cells.shape[dim], axis=dim)
        cells = jnp.concatenate(
            [
                lax.ppermute(tail, axis, [(i, (i + 1) % count) for i in range(ends)]),
                cells,
                lax.ppermute(head, axis, [((i + 1) % count, i) for i in range(ends)]),
            ],
            axis=dim,
        )
    return cells


def swapped(block, axis, apart):
    count = lax.axis_size(axis)
    route = []
    for low in range(count):
        high = low | 1 << apart
        if high != low and high < count:
            route += [(low, high), (high, low)]
    return lax.ppermute(block, axis, route)


def pair_mean(stacked):
    wide = stacked.astype(jnp.float32).reshape(
        stacked.shape[0], stacked.shape[1] // 2, 2, stacked.shape[2]
    )
    return ((wide[:, :, 0] + wide[:, :, 1]) * 0.5).astype(jnp.bfloat16)


def neighbor(payload, offset):
    return shifted(payload, "seq", offset)


def giveback(payload, offset):
    return shifted(payload, "seq", offset)


def return_fine(payload, offset):
    return shifted(payload, "seq", offset)


def body(queries, key_input, value_input, cotangent):
    seq_count = lax.axis_size("seq")
    device_pos = lax.axis_index("seq")
    row_count, feat_width = queries.shape
    scale = HEAD_DIM ** (-0.5)
    query_heads = queries.reshape(row_count, HEADS, HEAD_DIM)
    grad_heads = cotangent.reshape(row_count, HEADS, HEAD_DIM)
    stacked = jnp.stack([key_input, value_input])
    first_level = pair_mean(stacked)
    fine_keys = with_halo(stacked, (("seq", 1),), BLOCK)
    prev_block = neighbor(first_level, 1)
    next_block = neighbor(first_level, -1)
    key_sets = [fine_keys, jnp.concatenate([prev_block, first_level, next_block], axis=1)]
    current = first_level
    height = 2
    stride = 1 << height - 1
    own_half = pair_mean(current)
    partner = swapped(own_half, "seq", height - 2)
    is_upper = device_pos >> height - 2 & 1 == 1
    current = jnp.where(
        is_upper,
        jnp.concatenate([partner, own_half], axis=1),
        jnp.concatenate([own_half, partner], axis=1),
    )
    key_sets.append(
        jnp.concatenate([neighbor(current, stride), current, neighbor(current, -stride)], axis=1)
    )
    row_block = (jnp.arange(row_count) // BLOCK)[:, None]
    fine_cols = (jnp.arange(row_count + 2 * BLOCK) // BLOCK)[None, :]
    last_block = row_count // BLOCK + 1
    fine_mask = (
        (fine_cols >= row_block)
        & (fine_cols <= row_block + 2)
        & ((fine_cols != 0) | (device_pos >= 1))
        & ((fine_cols != last_block) | (device_pos < seq_count - 1))
    )
    col_block = jnp.arange(3 * BLOCK) // BLOCK
    score_list = []
    for height in range(LEVELS):
        key_rows = key_sets[height][0].reshape(-1, HEADS, HEAD_DIM)
        scores = (
            jnp.einsum("qhd,khd->hqk", query_heads, key_rows, preferred_element_type=jnp.float32)
            * scale
            + height * log_two
        )
        if height == 0:
            valid_mask = fine_mask[None, :, :]
        else:
            stride = 1 << height - 1
            valid_mask = (
                (col_block == 1)
                | (col_block == 0) & (device_pos >= stride)
                | (col_block == 2) & (device_pos + stride < seq_count)
            )[None, None, :]
        score_list.append(jnp.where(valid_mask, scores, masked_score))
    largest = functools.reduce(jnp.maximum, [jnp.max(s, axis=-1) for s in score_list])
    totals = functools.reduce(
        jnp.add, [jnp.sum(jnp.exp(s - largest[..., None]), axis=-1) for s in score_list]
    )
    log_total = largest + jnp.log(totals)
    weight_list = [jnp.exp(s - log_total[..., None]) for s in score_list]
    rounded_list = [w.astype(jnp.bfloat16) for w in weight_list]
    output = jnp.zeros((row_count, HEADS, HEAD_DIM), jnp.float32)
    for height in range(LEVELS):
        value_rows = key_sets[height][1].reshape(-1, HEADS, HEAD_DIM)
        output = output + jnp.einsum(
            "hqk,khd->qhd", rounded_list[height], value_rows, preferred_element_type=jnp.float32
        )
    attended = output.reshape(row_count, feat_width).astype(jnp.bfloat16)
    row_dots = jnp.sum(
        grad_heads.astype(jnp.float32)
        * attended.reshape(row_count, HEADS, HEAD_DIM).astype(jnp.float32),
        axis=-1,
    ).T
    grad_q = jnp.zeros((row_count, HEADS, HEAD_DIM), jnp.float32)
    level_grads = []
    for height in range(LEVELS):
        key_rows = key_sets[height][0].reshape(-1, HEADS, HEAD_DIM)
        value_rows = key_sets[height][1].reshape(-1, HEADS, HEAD_DIM)
        grad_weights = jnp.einsum(
            "qhd,khd->hqk", grad_heads, value_rows, preferred_element_type=jnp.float32
        )
        grad_scores = (weight_list[height] * (grad_weights - row_dots[..., None]) * scale).astype(
            jnp.bfloat16
        )
        grad_q = grad_q + jnp.einsum(
            "hqk,khd->qhd", grad_scores, key_rows, preferred_element_type=jnp.float32
        )
        key_part = jnp.einsum(
            "hqk,qhd->khd", grad_scores, query_heads, preferred_element_type=jnp.float32
        )
        value_part = jnp.einsum(
            "hqk,qhd->khd", rounded_list[height], grad_heads, preferred_element_type=jnp.float32
        )
        level_grads.append(jnp.stack([key_part, value_part]).reshape(2, -1, feat_width))
    fine_rows = level_grads[0]
    tail_part = return_fine(fine_rows[:, :BLOCK], -1)
    head_part = return_fine(fine_rows[:, row_count + BLOCK :], 1)
    fine_grads = fine_rows[:, BLOCK : BLOCK + row_count]
    fine_grads = fine_grads + jnp.pad(head_part, ((0, 0), (0, row_count - BLOCK), (0, 0)))
    fine_grads = fine_grads + jnp.pad(tail_part, ((0, 0), (row_count - BLOCK, 0), (0, 0)))
    for height in range(1, LEVELS):
        stride = 1 << height - 1
        grads = level_grads[height].reshape(2, 3, BLOCK, feat_width)
        for bit_no in range(height - 2, -1, -1):
            length = grads.shape[2]
            is_upper = device_pos >> bit_no & 1 == 1
            lower_part = grads[:, :, : length // 2]
            upper_part = grads[:, :, length // 2 :]
            sent_part = jnp.where(is_upper, lower_part, upper_part)
            grads = jnp.where(is_upper, upper_part, lower_part) + swapped(sent_part, "seq", bit_no)
        shares = grads[:, 1] + giveback(grads[:, 0], -stride) + giveback(grads[:, 2], stride)
        fine_grads = fine_grads + jnp.repeat(shares, 1 << height, axis=1) * 0.5**height
    grad_queries = grad_q.reshape(row_count, feat_width).astype(jnp.bfloat16)
    return (
        attended,
        grad_queries,
        fine_grads[0].astype(jnp.bfloat16),
        fine_grads[1].astype(jnp.bfloat16),
    )


def solution(mesh):
    return jax.shard_map(
        body,
        mesh=mesh,
        in_specs=(
            P(("groups", "seq"), None),
            P(("groups", "seq"), None),
            P(("groups", "seq"), None),
            P(("groups", "seq"), None),
        ),
        out_specs=(
            P(("groups", "seq"), None),
            P(("groups", "seq"), None),
            P(("groups", "seq"), None),
            P(("groups", "seq"), None),
        ),
        check_vma=False,
    )
```

profile of v0, /device:TPU:21, one launch (start us, length us, event | category | flops | bytes accessed | tf_op | source)
XLA Modules:
  0.0 202.5 jit_solution(1339056079182594805)
XLA Ops:
  4.8 3.9 %convert_reduce_fusion = (f32[2,64,2048]{2,1,0:T(8,128)S(1)}, bf16[2,64,1,2048]{3,2,1,0:T(2,128)(2,1)S(1)}) fusion(f32[2,64,2,2048]{3,2,1,0:T(2,128)S(1)} %maximum_convert_fusion), kind=kLoop, calls=%fused_computation.67 | loop fusion | flops 1048576 | bytes 3670016 | tf_op jit(solution)/shard_map/convert_element_type | solution.py:53
  12.4 3.9 %collective-permute-start.2 = (bf16[2,64,2048]{2,1,0:T(8,128)(2,1)}, bf16[2,64,2048]{2,1,0:T(8,128)(2,1)}, u32[]{:S(2)}, u32[]{:S(2)}) collective-permute-start(bf16[2,64,2048]{2,1,0:T(8,128)(2,1)} %bitcast.192), channel_id=1, source_target_pairs={{0,1},{1,2},{2,3},{3,4},{4,5},{5,6},{6,7},{7,8},{8,9},{9,10},{10,1... | collective-permute-start | bytes 1572872 | tf_op jit(solution)/shard_map/ppermute | solution.py:22
  26.0 4.1 %collective-permute-start = (bf16[2,64,2048]{2,1,0:T(8,128)(2,1)}, bf16[2,64,2048]{2,1,0:T(8,128)(2,1)}, u32[]{:S(2)}, u32[]{:S(2)}) collective-permute-start(bf16[2,64,2048]{2,1,0:T(8,128)(2,1)} %copy.117), channel_id=1, source_target_pairs={{0,1},{1,2},{2,3},{3,4},{4,5},{5,6},{6,7},{7,8},{8,9},{9,10},{10,1... | collective-permute-start | bytes 1572872 | tf_op jit(solution)/shard_map/ppermute | solution.py:33
  35.5 4.4 %collective-permute-start.5 = (bf16[2,64,2048]{2,1,0:T(8,128)(2,1)}, bf16[2,64,2048]{2,1,0:T(8,128)(2,1)}, u32[]{:S(2)}, u32[]{:S(2)}) collective-permute-start(bf16[2,64,2048]{2,1,0:T(8,128)(2,1)} %maximum_select_fusion), channel_id=1, source_target_pairs={{0,2},{1,3},{2,4},{3,5},{4,6},{5,7},{6,8},{7,9},{8,10},{9,11},{10,... | collective-permute-start | bytes 1572872 | tf_op jit(solution)/shard_map/ppermute | solution.py:22
  52.3 6.7 %collective-permute-done.6 = bf16[2,64,2048]{2,1,0:T(8,128)(2,1)} collective-permute-done((bf16[2,64,2048]{2,1,0:T(8,128)(2,1)}, bf16[2,64,2048]{2,1,0:T(8,128)(2,1)}, u32[]{:S(2)}, u32[]{:S(2)}) %collective-permute-start.6) | collective-permute-done | bytes 524320 | tf_op jit(solution)/shard_map/ppermute | solution.py:22
  59.0 3.3 %collective-permute-done.5 = bf16[2,64,2048]{2,1,0:T(8,128)(2,1)} collective-permute-done((bf16[2,64,2048]{2,1,0:T(8,128)(2,1)}, bf16[2,64,2048]{2,1,0:T(8,128)(2,1)}, u32[]{:S(2)}, u32[]{:S(2)}) %collective-permute-start.5) | collective-permute-done | bytes 524320 | tf_op jit(solution)/shard_map/ppermute | solution.py:22
  80.5 2.6 %stack.54 = f32[1,3,64,2048]{3,2,1,0:T(8,128)} reshape(f32[192,16,128]{2,1,0:T(8,128)} %copy.154) | data formatting | bytes 3145728 | tf_op jit(solution)/shard_map/stack | solution.py:165
  83.2 2.9 %constant_dynamic-update-slice_fusion.3 = f32[2,3,64,2048]{3,2,1,0:T(8,128)} fusion(f32[1,3,64,2048]{3,2,1,0:T(8,128)} %stack.54), kind=kLoop, calls=%fused_computation.116 | loop fusion | bytes 3145728
  90.8 2.7 %constant_dynamic-update-slice_fusion.2 = f32[2,3,64,2048]{3,2,1,0:T(8,128)} fusion(f32[2,3,64,2048]{3,2,1,0:T(8,128)} %constant_dynamic-update-slice_fusion.3, f32[1,3,64,2048]{3,2,1,0:T(8,128)} %stack.55), kind=kLoop, calls=%fused_computation.115 | loop fusion | bytes 3145728 | tf_op jit(solution)/shard_map/stack | solution.py:165
  93.5 3.4 %slice_select_fusion = f32[2,3,32,2048]{3,2,1,0:T(8,128)} fusion(f32[2,3,64,2048]{3,2,1,0:T(8,128)} %constant_dynamic-update-slice_fusion.2, pred[]{:T(512)S(6)} %eq.46), kind=kLoop, calls=%fused_computation.45 | loop fusion | flops 393216 | bytes 4718593 | tf_op jit(solution)/shard_map/jit(_where)/select_n | solution.py:180
  98.9 2.6 %stack.51 = f32[1,3,64,2048]{3,2,1,0:T(8,128)} reshape(f32[192,16,128]{2,1,0:T(8,128)} %copy.148) | data formatting | bytes 3145728 | tf_op jit(solution)/shard_map/stack | solution.py:165
  101.6 2.8 %constant_dynamic-update-slice_fusion.1 = f32[2,3,64,2048]{3,2,1,0:T(8,128)} fusion(f32[1,3,64,2048]{3,2,1,0:T(8,128)} %stack.51), kind=kLoop, calls=%fused_computation.114 | loop fusion | bytes 3145728
  109.1 2.8 %constant_dynamic-update-slice_fusion = f32[2,3,64,2048]{3,2,1,0:T(8,128)} fusion(f32[2,3,64,2048]{3,2,1,0:T(8,128)} %constant_dynamic-update-slice_fusion.1, f32[1,3,64,2048]{3,2,1,0:T(8,128)} %stack.52), kind=kLoop, calls=%fused_computation.113 | loop fusion | bytes 3145728 | tf_op jit(solution)/shard_map/stack | solution.py:165
  116.0 3.2 %slice_bitcast_fusion.1 = (f32[2,64,2048]{2,1,0:T(8,128)}, f32[2,64,2048]{2,1,0:T(8,128)}) fusion(f32[2,3,64,2048]{3,2,1,0:T(8,128)} %constant_dynamic-update-slice_fusion), kind=kLoop, calls=%fused_computation.56 | loop fusion | bytes 4194304 | tf_op jit(solution)/shard_map/squeeze | solution.py:182
  125.4 2.9 %copy.145 = f32[1,256,2048]{2,1,0:T(8,128)} copy(f32[1,256,2048]{1,2,0:T(8,128)} %bitcast.203) | data formatting | bytes 4194304 | tf_op jit(solution)/shard_map/stack | solution.py:165
  130.1 3.1 %copy.146 = f32[1,256,2048]{2,1,0:T(8,128)} copy(f32[1,256,2048]{1,2,0:T(8,128)} %bitcast.204) | data formatting | bytes 4194304 | tf_op jit(solution)/shard_map/stack | solution.py:165
  133.2 2.8 %fusion.23 = (f32[2,64,2048]{2,1,0:T(8,128)}, f32[2,64,2048]{2,1,0:T(8,128)}) fusion(f32[1,256,2048]{2,1,0:T(8,128)S(1)} %copy-done.2, f32[1,256,2048]{2,1,0:T(8,128)} %copy.146), kind=kLoop, calls=%fused_computation.54 | loop fusion | flops 524288 | bytes 6291456 | tf_op jit(solution)/shard_map/stack | solution.py:165
  136.1 3.6 %collective-permute-start.8 = (f32[2,64,2048]{2,1,0:T(8,128)}, f32[2,64,2048]{2,1,0:T(8,128)}, u32[]{:S(2)}, u32[]{:S(2)}) collective-permute-start(f32[2,64,2048]{2,1,0:T(8,128)} %get-tuple-element.25), channel_id=1, source_target_pairs={{1,0},{2,1},{3,2},{4,3},{5,4},{6,5},{7,6},{8,7},{9,8},{10,9},{11,1... | collective-permute-start | bytes 3145736 | tf_op jit(solution)/shard_map/ppermute | solution.py:22
  139.7 2.8 %collective-permute-start.7 = (f32[2,64,2048]{2,1,0:T(8,128)}, f32[2,64,2048]{2,1,0:T(8,128)}, u32[]{:S(2)}, u32[]{:S(2)}) collective-permute-start(f32[2,64,2048]{2,1,0:T(8,128)} %get-tuple-element.24), channel_id=1, source_target_pairs={{0,1},{1,2},{2,3},{3,4},{4,5},{5,6},{6,7},{7,8},{8,9},{9,10},{10,1... | collective-permute-start | bytes 3145736 | tf_op jit(solution)/shard_map/ppermute | solution.py:22
  148.5 20.8 %collective-permute-start.12 = (f32[2,32,2048]{2,1,0:T(8,128)}, f32[2,32,2048]{2,1,0:T(8,128)}, u32[]{:S(2)}, u32[]{:S(2)}) collective-permute-start(f32[2,32,2048]{2,1,0:T(8,128)} %get-tuple-element.30), channel_id=1, source_target_pairs={{2,0},{3,1},{4,2},{5,3},{6,4},{7,5},{8,6},{9,7},{10,8},{11,9},{12,... | collective-permute-start | bytes 1572872 | tf_op jit(solution)/shard_map/ppermute | solution.py:22
  173.9 3.7 %mul.88 = f32[2,128,2048]{2,1,0:T(8,128)} reshape(f32[2,64,2,2048]{3,2,1,0:T(2,128)} %broadcast_in_dim.55) | data formatting | bytes 4194304 | tf_op jit(solution)/shard_map/mul | solution.py:183
  177.5 14.0 %collective-permute-done.13 = f32[2,32,2048]{2,1,0:T(8,128)S(1)} collective-permute-done((f32[2,32,2048]{2,1,0:T(8,128)}, f32[2,32,2048]{2,1,0:T(8,128)S(1)}, u32[]{:S(2)}, u32[]{:S(2)}) %collective-permute-start.13) | collective-permute-done | bytes 524320 | tf_op jit(solution)/shard_map/ppermute | solution.py:22
  194.7 3.0 %mul.91 = f32[2,128,2048]{2,1,0:T(8,128)} reshape(f32[2,32,4,2048]{3,2,1,0:T(4,128)} %broadcast_in_dim.56) | data formatting | bytes 4194304 | tf_op jit(solution)/shard_map/mul | solution.py:183
  197.7 3.8 %fusion.5 = bf16[2,128,2048]{2,1,0:T(8,128)(2,1)S(1)} fusion(f32[2,128,2048]{2,1,0:T(8,128)} %mul.91, f32[2,128,2048]{2,1,0:T(8,128)} %mul.88, f32[1,256,2048]{2,1,0:T(8,128)S(1)} %copy-done.2, f32[1,256,2048]{2,1,0:T(8,128)} %copy.146, f32[2,64,2048]{2,1,0:T(8,128)} %collective-permute-done.8, f32[2,64,2048]{2,1,0:T(8,128)} %collective-permute-done.7), kind=kLoop, calls=%fused_computation.9 | loop fusion | flops 3145728 | bytes 11534336 | tf_op jit(solution)/shard_map/convert.3
  (114 shorter events, 91.6 us)
Async XLA Ops:
  0.6 49.5 %copy-start = (bf16[128,2048]{1,0:T(8,128)(2,1)S(1)}, bf16[128,2048]{1,0:T(8,128)(2,1)}, u32[]{:S(2)}) copy-start(bf16[128,2048]{1,0:T(8,128)(2,1)} %param.4) | copy-start | bytes 1572868
  9.8 25.7 %collective-permute-start.3 = (bf16[2,64,2048]{2,1,0:T(8,128)(2,1)}, bf16[2,64,2048]{2,1,0:T(8,128)(2,1)}, u32[]{:S(2)}, u32[]{:S(2)}) collective-permute-start(bf16[2,64,2048]{2,1,0:T(8,128)(2,1)} %bitcast.192), channel_id=1, source_target_pairs={{1,0},{2,1},{3,2},{4,3},{5,4},{6,5},{7,6},{8,7},{9,8},{10,9},{11,1... | collective-permute-start | bytes 1572872 | tf_op jit(solution)/shard_map/ppermute | solution.py:22
  12.4 27.6 %collective-permute-start.2 = (bf16[2,64,2048]{2,1,0:T(8,128)(2,1)}, bf16[2,64,2048]{2,1,0:T(8,128)(2,1)}, u32[]{:S(2)}, u32[]{:S(2)}) collective-permute-start(bf16[2,64,2048]{2,1,0:T(8,128)(2,1)} %bitcast.192), channel_id=1, source_target_pairs={{0,1},{1,2},{2,3},{3,4},{4,5},{5,6},{6,7},{7,8},{8,9},{9,10},{10,1... | collective-permute-start | bytes 1572872 | tf_op jit(solution)/shard_map/ppermute | solution.py:22
  16.9 1.3 copy-start.11
  16.9 1.6 copy-start.12
  18.1 13.5 %collective-permute-start.4 = (bf16[2,32,2048]{2,1,0:T(8,128)(2,1)S(1)}, bf16[2,32,2048]{2,1,0:T(8,128)(2,1)}, u32[]{:S(2)}, u32[]{:S(2)}) collective-permute-start(bf16[2,32,2048]{2,1,0:T(8,128)(2,1)S(1)} %fusion.54), channel_id=1, source_target_pairs={{0,1},{1,0},{2,3},{3,2},{4,5},{5,4},{6,7},{7,6},{8,9},{9,8},{10,11... | collective-permute-start | bytes 786440 | tf_op jit(solution)/shard_map/ppermute | solution.py:49
  22.4 21.2 %collective-permute-start.1 = (bf16[2,64,2048]{2,1,0:T(8,128)(2,1)}, bf16[2,64,2048]{2,1,0:T(8,128)(2,1)}, u32[]{:S(2)}, u32[]{:S(2)}) collective-permute-start(bf16[2,64,2048]{2,1,0:T(8,128)(2,1)} %copy.118), channel_id=1, source_target_pairs={{1,0},{2,1},{3,2},{4,3},{5,4},{6,5},{7,6},{8,7},{9,8},{10,9},{11,1... | collective-permute-start | bytes 1572872 | tf_op jit(solution)/shard_map/ppermute | solution.py:35
  26.0 19.2 %collective-permute-start = (bf16[2,64,2048]{2,1,0:T(8,128)(2,1)}, bf16[2,64,2048]{2,1,0:T(8,128)(2,1)}, u32[]{:S(2)}, u32[]{:S(2)}) collective-permute-start(bf16[2,64,2048]{2,1,0:T(8,128)(2,1)} %copy.117), channel_id=1, source_target_pairs={{0,1},{1,2},{2,3},{3,4},{4,5},{5,6},{6,7},{7,8},{8,9},{9,10},{10,1... | collective-permute-start | bytes 1572872 | tf_op jit(solution)/shard_map/ppermute | solution.py:33
  33.6 25.4 %collective-permute-start.6 = (bf16[2,64,2048]{2,1,0:T(8,128)(2,1)}, bf16[2,64,2048]{2,1,0:T(8,128)(2,1)}, u32[]{:S(2)}, u32[]{:S(2)}) collective-permute-start(bf16[2,64,2048]{2,1,0:T(8,128)(2,1)} %maximum_select_fusion), channel_id=1, source_target_pairs={{2,0},{3,1},{4,2},{5,3},{6,4},{7,5},{8,6},{9,7},{10,8},{11,9},{12,... | collective-permute-start | bytes 1572872 | tf_op jit(solution)/shard_map/ppermute | solution.py:22
  35.5 26.7 %collective-permute-start.5 = (bf16[2,64,2048]{2,1,0:T(8,128)(2,1)}, bf16[2,64,2048]{2,1,0:T(8,128)(2,1)}, u32[]{:S(2)}, u32[]{:S(2)}) collective-permute-start(bf16[2,64,2048]{2,1,0:T(8,128)(2,1)} %maximum_select_fusion), channel_id=1, source_target_pairs={{0,2},{1,3},{2,4},{3,5},{4,6},{5,7},{6,8},{7,9},{8,10},{9,11},{10,... | collective-permute-start | bytes 1572872 | tf_op jit(solution)/shard_map/ppermute | solution.py:22
  70.2 6.3 %copy-start.3 = (bf16[16,128,256]{1,2,0:T(8,128)(2,1)}, bf16[16,128,256]{1,2,0:T(8,128)(2,1)S(1)}, u32[]{:S(2)}) copy-start(bf16[16,128,256]{1,2,0:T(8,128)(2,1)S(1)} %fusion.7) | copy-start | bytes 3145732
  83.2 2.9 %copy-start.7 = (f32[192,16,128]{2,0,1:T(8,128)S(1)}, f32[192,16,128]{2,0,1:T(8,128)}, u32[]{:S(2)}) copy-start(f32[192,16,128]{2,0,1:T(8,128)} %convolution_bitcast_fusion) | copy-start | bytes 4718596
  93.5 3.4 %copy-start.8 = (f32[192,16,128]{2,0,1:T(8,128)S(1)}, f32[192,16,128]{2,0,1:T(8,128)}, u32[]{:S(2)}) copy-start(f32[192,16,128]{2,0,1:T(8,128)} %convolution_bitcast_fusion.3) | copy-start | bytes 4718596
  96.9 45.7 %collective-permute-start.11 = (f32[2,3,32,2048]{3,2,1,0:T(8,128)}, f32[2,3,32,2048]{3,2,1,0:T(8,128)}, u32[]{:S(2)}, u32[]{:S(2)}) collective-permute-start(f32[2,3,32,2048]{3,2,1,0:T(8,128)} %slice_select_fusion), channel_id=1, source_target_pairs={{0,1},{1,0},{2,3},{3,2},{4,5},{5,4},{6,7},{7,6},{8,9},{9,8},{10,11... | collective-permute-start | bytes 4718600 | tf_op jit(solution)/shard_map/ppermute | solution.py:49
  101.6 2.8 %copy-start.6 = (f32[192,16,128]{2,0,1:T(8,128)S(1)}, f32[192,16,128]{2,0,1:T(8,128)}, u32[]{:S(2)}) copy-start(f32[192,16,128]{2,0,1:T(8,128)} %convolution_bitcast_fusion.2) | copy-start | bytes 4718596
  116.0 7.6 %copy-start.4 = (bf16[16,128,256]{1,2,0:T(8,128)(2,1)S(1)}, bf16[16,128,256]{1,2,0:T(8,128)(2,1)}, u32[]{:S(2)}) copy-start(bf16[16,128,256]{1,2,0:T(8,128)(2,1)} %copy-done.3) | copy-start | bytes 3145732
  119.2 29.3 %collective-permute-start.10 = (f32[2,64,2048]{2,1,0:T(8,128)}, f32[2,64,2048]{2,1,0:T(8,128)}, u32[]{:S(2)}, u32[]{:S(2)}) collective-permute-start(f32[2,64,2048]{2,1,0:T(8,128)} %get-tuple-element.27), channel_id=1, source_target_pairs={{0,1},{1,2},{2,3},{3,4},{4,5},{5,6},{6,7},{7,8},{8,9},{9,10},{10,1... | collective-permute-start | bytes 3145736 | tf_op jit(solution)/shard_map/ppermute | solution.py:22
  121.2 48.1 %collective-permute-start.9 = (f32[2,64,2048]{2,1,0:T(8,128)}, f32[2,64,2048]{2,1,0:T(8,128)}, u32[]{:S(2)}, u32[]{:S(2)}) collective-permute-start(f32[2,64,2048]{2,1,0:T(8,128)} %get-tuple-element.26), channel_id=1, source_target_pairs={{1,0},{2,1},{3,2},{4,3},{5,4},{6,5},{7,6},{8,7},{9,8},{10,9},{11,1... | collective-permute-start | bytes 3145736 | tf_op jit(solution)/shard_map/ppermute | solution.py:22
  130.1 3.1 %copy-start.2 = (f32[1,256,2048]{2,1,0:T(8,128)S(1)}, f32[1,256,2048]{2,1,0:T(8,128)}, u32[]{:S(2)}) copy-start(f32[1,256,2048]{2,1,0:T(8,128)} %copy.145) | copy-start | bytes 6291460
  133.2 9.3 %copy-start.1 = (f32[2,3,64,2048]{3,2,1,0:T(8,128)S(1)}, f32[2,3,64,2048]{3,2,1,0:T(8,128)}, u32[]{:S(2)}) copy-start(f32[2,3,64,2048]{3,2,1,0:T(8,128)} %constant_dynamic-update-slice_fusion.2) | copy-start | bytes 9437188
  136.1 61.6 %collective-permute-start.8 = (f32[2,64,2048]{2,1,0:T(8,128)}, f32[2,64,2048]{2,1,0:T(8,128)}, u32[]{:S(2)}, u32[]{:S(2)}) collective-permute-start(f32[2,64,2048]{2,1,0:T(8,128)} %get-tuple-element.25), channel_id=1, source_target_pairs={{1,0},{2,1},{3,2},{4,3},{5,4},{6,5},{7,6},{8,7},{9,8},{10,9},{11,1... | collective-permute-start | bytes 3145736 | tf_op jit(solution)/shard_map/ppermute | solution.py:22
  139.7 58.0 %collective-permute-start.7 = (f32[2,64,2048]{2,1,0:T(8,128)}, f32[2,64,2048]{2,1,0:T(8,128)}, u32[]{:S(2)}, u32[]{:S(2)}) collective-permute-start(f32[2,64,2048]{2,1,0:T(8,128)} %get-tuple-element.24), channel_id=1, source_target_pairs={{0,1},{1,2},{2,3},{3,4},{4,5},{5,6},{6,7},{7,8},{8,9},{9,10},{10,1... | collective-permute-start | bytes 3145736 | tf_op jit(solution)/shard_map/ppermute | solution.py:22
  146.6 44.9 %collective-permute-start.13 = (f32[2,32,2048]{2,1,0:T(8,128)}, f32[2,32,2048]{2,1,0:T(8,128)S(1)}, u32[]{:S(2)}, u32[]{:S(2)}) collective-permute-start(f32[2,32,2048]{2,1,0:T(8,128)} %get-tuple-element.31), channel_id=1, source_target_pairs={{0,2},{1,3},{2,4},{3,5},{4,6},{5,7},{6,8},{7,9},{8,10},{9,11},{10,... | collective-permute-start | bytes 1572872 | tf_op jit(solution)/shard_map/ppermute | solution.py:22
  148.5 43.0 %collective-permute-start.12 = (f32[2,32,2048]{2,1,0:T(8,128)}, f32[2,32,2048]{2,1,0:T(8,128)}, u32[]{:S(2)}, u32[]{:S(2)}) collective-permute-start(f32[2,32,2048]{2,1,0:T(8,128)} %get-tuple-element.30), channel_id=1, source_target_pairs={{2,0},{3,1},{4,2},{5,3},{6,4},{7,5},{8,6},{9,7},{10,8},{11,9},{12,... | collective-permute-start | bytes 1572872 | tf_op jit(solution)/shard_map/ppermute | solution.py:22
  (3 other events, 3.5 us)
where the time goes:
time: 204 us; the launch traced here: 202 us
  local copies, waits for them, and re-layouts  77 us (38%)
  starting transfers between devices  52.8 us (26%)
  other arithmetic  30.2 us (15%)
  waiting for transfers between devices  23.9 us (12%)
  matrix products  17.3 us (8%)
    ppermute x10, starting transfers between devices, shifted(): lax.ppermute(value, axis, [(source, source + steps) for source in range(i...  46.3 us
    ppermute x10, waiting for transfers between devices, shifted(): lax.ppermute(value, axis, [(source, source + steps) for source in range(i...  23.9 us
    another operation x8, local copies, waits for them, and re-layouts, body(): jnp.stack([key_part, value_part]).reshape(2, -1, feat_width)  21.9 us
    unnamed x40, local copies, waits for them, and re-layouts  18.2 us
    mul x2, local copies, waits for them, and re-layouts, body(): jnp.repeat(shares, 1 << height, axis=1) * 0.5 ** height  6.61 us
    convert_element_type x2, other arithmetic, pair_mean(): stacked.astype(jnp.float32)  5.2 us
    dot_general x3, matrix products, body(): jnp.einsum('hqk,qhd->khd', rounded_list[height], grad_heads, preferred_el...  5.1 us
    broadcast_in_dim x2, local copies, waits for them, and re-layouts, body(): jnp.repeat(shares, 1 << height, axis=1) * 0.5 ** height  4.45 us
  transfers between devices with their start and end apart: 14, of which 3 were waited for; matrix products, arithmetic and copies ran while one was open for 36% of the time, Pallas kernels for 0%

commit v1 on v0

v1 whole, which is shorter than its diff:
```python
import math

import jax
import jax.numpy as jnp
from jax import lax
from jax.experimental import pallas as pl
from jax.experimental.pallas import tpu as pltpu
from jax.sharding import PartitionSpec as P

HEADS = 16
HEAD_DIM = 128
BLOCK = 64
HALF = BLOCK // 2
CHUNKS = 4

SIB_FINE = 2 * BLOCK
OUT_FINE = SIB_FINE + BLOCK
OWN_L1 = OUT_FINE + BLOCK
OWN_L2 = OWN_L1 + BLOCK
SIB_L1 = OWN_L2 + HALF
SIB_L2 = SIB_L1 + BLOCK
OUT_L1 = SIB_L2 + HALF
OUT_L2 = OUT_L1 + BLOCK
FAR_L2 = OUT_L2 + BLOCK
CAND = FAR_L2 + BLOCK
COARSE = BLOCK + HALF
BACK = BLOCK + COARSE + BLOCK
FWD = BLOCK + HALF + HALF

masked_score = -1e30
MESH = pl.DeviceIdType.MESH


def nt(a, b):
    return lax.dot_general(a, b, (((1,), (1,)), ((), ())), preferred_element_type=jnp.float32)


def nn(a, b):
    return lax.dot_general(a, b, (((1,), (0,)), ((), ())), preferred_element_type=jnp.float32)


def tn(a, b):
    return lax.dot_general(a, b, (((0,), (0,)), ((), ())), preferred_element_type=jnp.float32)


def pool_matrix(rows):
    row = lax.broadcasted_iota(jnp.int32, (rows // 2, rows), 0)
    col = lax.broadcasted_iota(jnp.int32, (rows // 2, rows), 1)
    return jnp.where((col >> 1) == row, 0.5, 0.0).astype(jnp.bfloat16)


def spread_matrix(rows):
    row = lax.broadcasted_iota(jnp.int32, (2 * rows, rows), 0)
    col = lax.broadcasted_iota(jnp.int32, (2 * rows, rows), 1)
    return jnp.where((row >> 1) == col, 0.5, 0.0).astype(jnp.bfloat16)


def pooled(rows):
    return nn(pool_matrix(rows.shape[0]), rows).astype(jnp.bfloat16)


def spread(grads):
    matrix = spread_matrix(grads.shape[0])
    high = grads.astype(jnp.bfloat16)
    low = (grads - high.astype(jnp.float32)).astype(jnp.bfloat16)
    return nn(matrix, high) + nn(matrix, low)


def kernel(q_ref, k_ref, v_ref, do_ref, att_ref, gq_ref, gk_ref, gv_ref,
           kv, grad, bias, back_out, back_in, ret_out, ret_in, last_in, send_sem, recv_sem):
    count = lax.axis_size("seq")
    me = lax.axis_index("seq")
    side = lax.rem(me, 2)
    sib = me + 1 - 2 * side
    outer = me - 1 + 2 * side
    has_outer = (outer >= 0) & (outer < count)
    sib_outer = sib + 1 - 2 * side
    has_far = (sib_outer >= 0) & (sib_outer < count)
    feat = q_ref.shape[1]
    width = feat // CHUNKS
    scale = HEAD_DIM ** -0.5
    inner_start = pl.multiple_of(BLOCK * (1 - side), BLOCK)
    outer_start = pl.multiple_of(BLOCK * side, BLOCK)
    inner_half = pl.multiple_of(HALF * (1 - side), HALF)

    barrier = pltpu.get_barrier_semaphore()
    pl.semaphore_signal(barrier, inc=1, device_id={"seq": sib}, device_id_type=MESH)

    @pl.when(has_outer)
    def _():
        pl.semaphore_signal(barrier, inc=1, device_id={"seq": outer}, device_id_type=MESH)

    own = pl.ds(0, 2 * BLOCK)
    for which, ref in enumerate((k_ref, v_ref)):
        kv[which, own, :] = ref[...]
        first = pooled(ref[...])
        kv[which, OWN_L1:OWN_L1 + BLOCK, :] = first
        kv[which, OWN_L2:OWN_L2 + HALF, :] = pooled(first)

    @pl.when(jnp.logical_not(has_outer))
    def _():
        for which in range(2):
            kv[which, OUT_FINE:OUT_FINE + BLOCK, :] = jnp.zeros((BLOCK, feat), jnp.bfloat16)
            kv[which, OUT_L1:OUT_L1 + 2 * BLOCK, :] = jnp.zeros((2 * BLOCK, feat), jnp.bfloat16)

    lane = lax.broadcasted_iota(jnp.int32, (BLOCK, 2 * BLOCK), 1)
    is_outer_lane = (lane >> 6) == side
    zero = jnp.zeros((BLOCK, 2 * BLOCK), jnp.float32)
    bias[0:BLOCK] = zero
    bias[BLOCK:2 * BLOCK] = zero
    bias[SIB_FINE:SIB_FINE + BLOCK] = jnp.where(is_outer_lane, masked_score, zero)
    bias[OUT_FINE:OUT_FINE + BLOCK] = jnp.where(is_outer_lane & has_outer, zero, masked_score)
    bias[OWN_L1:OWN_L1 + BLOCK] = zero + 1.0
    bias[OWN_L2:OWN_L2 + HALF] = zero[:HALF] + 2.0
    bias[SIB_L1:SIB_L1 + BLOCK] = zero + 1.0
    bias[SIB_L2:SIB_L2 + HALF] = zero[:HALF] + 2.0
    bias[OUT_L1:OUT_L1 + BLOCK] = jnp.where(has_outer, zero + 1.0, masked_score)
    bias[OUT_L2:OUT_L2 + BLOCK] = jnp.where(has_outer, zero + 2.0, masked_score)
    bias[FAR_L2:FAR_L2 + BLOCK] = jnp.where(has_far, zero + 2.0, masked_score)

    @pl.when(has_outer)
    def _():
        pl.semaphore_wait(barrier, 2)

    @pl.when(jnp.logical_not(has_outer))
    def _():
        pl.semaphore_wait(barrier, 1)

    def part(ref, row, rows, chunk):
        return ref.at[:, pl.ds(row, rows), pl.ds(chunk * width, width)]

    def copy(stage, chunk, src, src_row, dst, dst_row, rows, target):
        return pltpu.make_async_remote_copy(
            src_ref=part(src, src_row, rows, chunk),
            dst_ref=part(dst, dst_row, rows, chunk),
            send_sem=send_sem.at[stage, chunk],
            recv_sem=recv_sem.at[stage, chunk],
            device_id={"seq": target},
            device_id_type=MESH,
        )

    def sib_fine(g):
        return copy(0, g, kv, inner_start, kv, SIB_FINE, BLOCK, sib)

    def sib_coarse(g):
        return copy(1, g, kv, OWN_L1, kv, SIB_L1, COARSE, sib)

    def out_fine(g):
        return copy(2, g, kv, outer_start, kv, OUT_FINE, BLOCK, outer)

    def out_l1(g):
        return copy(3, g, kv, OWN_L1 + inner_half, kv, OUT_L1 + HALF, HALF, outer)

    def out_l2(g):
        return copy(4, g, kv, SIB_L2, kv, OUT_L2 + HALF, HALF, outer)

    def far(g):
        return copy(5, g, kv, OUT_L2, kv, FAR_L2, BLOCK, sib)

    def back(g):
        return copy(6, g, back_out, 0, back_in, 0, BACK, sib)

    def ret(g):
        return copy(7, g, ret_out, 0, ret_in, 0, FWD, outer)

    def last(g):
        return copy(8, g, ret_in, BLOCK + HALF, last_in, 0, HALF, sib)

    for g in range(CHUNKS):
        sib_coarse(g).start()
        sib_fine(g).start()
    for g in range(CHUNKS):
        @pl.when(has_outer)
        def _():
            out_fine(g).start()
            out_l1(g).start()
        sib_coarse(g).wait_recv()

        @pl.when(has_outer)
        def _():
            out_l2(g).start()

    def relay_far(g):
        cols = pl.ds(g * width, width)

        @pl.when(has_outer)
        def _():
            out_fine(g).wait_recv()
            out_l1(g).wait_recv()
            out_l2(g).wait_recv()
            for which in range(2):
                first = pooled(kv[which, pl.ds(OUT_FINE, BLOCK), cols])
                kv[which, pl.ds(OUT_L1, HALF), cols] = first
                second = pooled(kv[which, pl.ds(OUT_L1, BLOCK), cols])
                kv[which, pl.ds(OUT_L2, HALF), cols] = second
        far(g).start()

    def attend(h):
        cols = pl.ds(pl.multiple_of(h * HEAD_DIM, HEAD_DIM), HEAD_DIM)
        q = q_ref[:, cols]
        do = do_ref[:, cols]
        k = kv[0, :, cols]
        v = kv[1, :, cols]
        scores = nt(k, q) * (scale * math.log2(math.e)) + bias[...]
        largest = jnp.max(scores, axis=0, keepdims=True)
        raised = jnp.exp2(scores - largest)
        weights = raised * (1.0 / jnp.sum(raised, axis=0, keepdims=True))
        weights_b = weights.astype(jnp.bfloat16)
        attended = tn(weights_b, v).astype(jnp.bfloat16)
        att_ref[:, cols] = attended
        product = do.astype(jnp.float32) * attended.astype(jnp.float32)
        row_dots = jnp.sum(product.T, axis=0, keepdims=True)
        grad_scores = (weights * (nt(v, do) - row_dots) * scale).astype(jnp.bfloat16)
        gq_ref[:, cols] = tn(grad_scores, k).astype(jnp.bfloat16)
        grad[0, :, cols] = nn(grad_scores, q)
        grad[1, :, cols] = nn(weights_b, do)

    def send_back(g):
        cols = pl.ds(g * width, width)
        for which in range(2):
            for dst, src, rows in ((0, SIB_FINE, BLOCK), (BLOCK, SIB_L1, COARSE),
                                   (BLOCK + COARSE, FAR_L2, BLOCK)):
                back_out[which, pl.ds(dst, rows), cols] = (
                    grad[which, pl.ds(src, rows), cols].astype(jnp.bfloat16))
        back(g).start()

    def send_outer(g):
        cols = pl.ds(g * width, width)
        back(g).wait_recv()
        for which in range(2):
            def take(row, rows):
                return back_in[which, pl.ds(row, rows), cols].astype(jnp.float32)
            rows = pl.ds(inner_start, BLOCK)
            grad[which, rows, cols] += take(0, BLOCK)
            rows = pl.ds(OWN_L1, COARSE)
            grad[which, rows, cols] += take(BLOCK, COARSE)

        @pl.when(has_outer)
        def _():
            for which in range(2):
                second = (grad[which, pl.ds(OUT_L2, BLOCK), cols]
                          + back_in[which, pl.ds(BLOCK + COARSE, BLOCK), cols].astype(jnp.float32))
                first = grad[which, pl.ds(OUT_L1, BLOCK), cols] + spread(second[:HALF])
                fine = grad[which, pl.ds(OUT_FINE, BLOCK), cols] + spread(first[:HALF])
                ret_out[which, pl.ds(0, BLOCK), cols] = fine.astype(jnp.bfloat16)
                ret_out[which, pl.ds(BLOCK, HALF), cols] = first[HALF:].astype(jnp.bfloat16)
                ret_out[which, pl.ds(BLOCK + HALF, HALF), cols] = second[HALF:].astype(jnp.bfloat16)
            ret(g).start()

    def take_outer(g):
        cols = pl.ds(g * width, width)

        @pl.when(has_outer)
        def _():
            ret(g).wait_recv()
            last(g).start()
            for which in range(2):
                rows = pl.ds(outer_start, BLOCK)
                grad[which, rows, cols] += ret_in[which, pl.ds(0, BLOCK), cols].astype(jnp.float32)
                rows = pl.ds(OWN_L1 + inner_half, HALF)
                grad[which, rows, cols] += ret_in[which, pl.ds(BLOCK, HALF), cols].astype(jnp.float32)

    def finish(g):
        cols = pl.ds(g * width, width)

        @pl.when(has_far)
        def _():
            last(g).wait_recv()
            for which in range(2):
                rows = pl.ds(OWN_L2, HALF)
                grad[which, rows, cols] += last_in[which, :, cols].astype(jnp.float32)
        for which, ref in enumerate((gk_ref, gv_ref)):
            first = grad[which, pl.ds(OWN_L1, BLOCK), cols] + spread(grad[which, pl.ds(OWN_L2, HALF), cols])
            fine = grad[which, pl.ds(0, 2 * BLOCK), cols] + spread(first)
            ref[:, cols] = fine.astype(jnp.bfloat16)

    heads = width // HEAD_DIM
    for g in range(CHUNKS):
        relay_far(g)
        sib_fine(g).wait_recv()
        far(g).wait_recv()
        lax.fori_loop(g * heads, (g + 1) * heads, lambda h, c: (attend(h), c)[1], 0)
        send_back(g)
        if g > 0:
            send_outer(g - 1)
    send_outer(CHUNKS - 1)
    for g in range(CHUNKS):
        take_outer(g)
        if g > 0:
            finish(g - 1)
    finish(CHUNKS - 1)
    for g in range(CHUNKS):
        for item in (sib_fine, sib_coarse, far, back):
            item(g).wait_send()

        @pl.when(has_outer)
        def _():
            for item in (out_fine, out_l1, out_l2, ret, last):
                item(g).wait_send()


def body(queries, key_input, value_input, cotangent):
    rows, feat = queries.shape
    out = jax.ShapeDtypeStruct((rows, feat), jnp.bfloat16)
    return tuple(pl.pallas_call(
        kernel,
        name="hier_attention",
        out_shape=[out] * 4,
        in_specs=[pl.BlockSpec(memory_space=pltpu.VMEM)] * 4,
        out_specs=[pl.BlockSpec(memory_space=pltpu.VMEM)] * 4,
        scratch_shapes=[
            pltpu.VMEM((2, CAND, feat), jnp.bfloat16),
            pltpu.VMEM((2, CAND, feat), jnp.float32),
            pltpu.VMEM((CAND, rows), jnp.float32),
            pltpu.VMEM((2, BACK, feat), jnp.bfloat16),
            pltpu.VMEM((2, BACK, feat), jnp.bfloat16),
            pltpu.VMEM((2, FWD, feat), jnp.bfloat16),
            pltpu.VMEM((2, FWD, feat), jnp.bfloat16),
            pltpu.VMEM((2, HALF, feat), jnp.bfloat16),
            pltpu.SemaphoreType.DMA((9, CHUNKS)),
            pltpu.SemaphoreType.DMA((9, CHUNKS)),
        ],
        compiler_params=pltpu.CompilerParams(
            collective_id=0, has_side_effects=True, vmem_limit_bytes=56 * 1024 * 1024),
    )(queries, key_input, value_input, cotangent))


def solution(mesh):
    spec = P(("groups", "seq"), None)
    return jax.shard_map(
        body, mesh=mesh, in_specs=(spec,) * 4, out_specs=(spec,) * 4, check_vma=False)
```

time: 204 us -> 67.8 us (0.33)
  local copies, waits for them, and re-layouts: 77 us -> 5.19 us
  Pallas kernels: 0 us -> 61.7 us
  starting transfers between devices: 52.8 us -> 0 us
  other arithmetic: 30.2 us -> 0 us
  waiting for transfers between devices: 23.9 us -> 0 us
  matrix products: 17.3 us -> 0 us
    pallas_call x0 -> x1, Pallas kernels: none -> 61.7 us  [body(): pl.pallas_call(kernel, name='hier_attention', out_shape=[out] * 4, in_spe...]
    ppermute x14 -> x0, starting transfers between devices: 52.8 us -> none  [the longest x10 46.3 us: shifted(): lax.ppermute(value, axis, [(source, source + steps) for source in range(i...]
    another operation x10 -> x0, local copies, waits for them, and re-layouts: 24.7 us -> none  [the longest x8 21.9 us: body(): jnp.stack([key_part, value_part]).reshape(2, -1, feat_width)]
    ppermute x14 -> x0, waiting for transfers between devices: 23.9 us -> none  [the longest x10 23.9 us: shifted(): lax.ppermute(value, axis, [(source, source + steps) for source in range(i...]
    dot_general x18 -> x0, matrix products: 17.3 us -> none  [the longest x3 5.1 us: body(): jnp.einsum('hqk,qhd->khd', rounded_list[height], grad_heads, preferred_el...]
    unnamed x40 -> x10, local copies, waits for them, and re-layouts: 18.2 us -> 5.19 us
    transpose x4 -> x0, local copies, waits for them, and re-layouts: 8.71 us -> none  [the longest x2 4.37 us: body(): jnp.einsum('hqk,qhd->khd', grad_scores, query_heads, preferred_element_ty...]
    another operation x3 -> x0, other arithmetic: 7.95 us -> none
  transfers between devices with their start and end apart: 14 -> 0, of which waited for: 3 -> 0; matrix products, arithmetic and copies ran while one was open for 36% -> 0% of each run, Pallas kernels for 0% -> 0%
where the time goes in v1:
time: 67.8 us; the launch traced here: 67.5 us
  Pallas kernels  61.7 us (91%)
  local copies, waits for them, and re-layouts  5.19 us (8%)
    pallas_call x1, Pallas kernels, body(): pl.pallas_call(kernel, name='hier_attention', out_shape=[out] * 4, in_spe...  61.7 us
    unnamed x10, local copies, waits for them, and re-layouts  5.19 us

profile of v1, /device:TPU:21, one launch (start us, length us, event | category | flops | bytes accessed | tf_op | source)
XLA Modules:
  0.0 67.5 jit_solution(14743637800915699414)
XLA Ops:
  0.6 61.7 %hier_attention.1 = (bf16[128,2048]{1,0:T(8,128)(2,1)}, bf16[128,2048]{1,0:T(8,128)(2,1)}, bf16[128,2048]{1,0:T(8,128)(2,1)}, bf16[128,2048]{1,0:T(8,128)(2,1)}) custom-call(bf16[128,2048]{1,0:T(8,128)(2,1)} %q_ref.1, bf16[128,2048]{1,0:T(8,128)(2,1)} %k_ref.1, bf16[128,2048]{1,0:T(8,128)(2,1)} %v_ref.1, bf16[128,2048]{1,0:T(8,128)(2,1)} %do_ref.1), custom_call_target="tpu_custom_call" | custom-call | tf_op jit(solution)/shard_map/hier_attention/pallas_call | solution.py:305
  62.3 0.0 copy-start.2
  62.3 1.9 %copy.12 = bf16[128,2048]{1,0:T(8,128)(2,1)} copy(bf16[128,2048]{1,0:T(8,128)(2,1)} %get-tuple-element.8) | data formatting | bytes 1048576
  64.3 0.0 copy-done.2
  64.3 0.0 copy-start.1
  64.3 0.8 %copy.13 = bf16[128,2048]{1,0:T(8,128)(2,1)} copy(bf16[128,2048]{1,0:T(8,128)(2,1)S(1)} %copy-done.2) | data formatting | bytes 1048576
  65.1 0.4 copy-done.1
  65.5 0.0 copy-start
  65.5 0.8 %copy.14 = bf16[128,2048]{1,0:T(8,128)(2,1)} copy(bf16[128,2048]{1,0:T(8,128)(2,1)S(1)} %copy-done.1) | data formatting | bytes 1048576
  66.3 0.4 copy-done
  66.7 0.8 %copy.15 = bf16[128,2048]{1,0:T(8,128)(2,1)} copy(bf16[128,2048]{1,0:T(8,128)(2,1)S(1)} %copy-done) | data formatting | bytes 1048576
Async XLA Ops:
  62.3 2.0 %copy-start.2 = (bf16[128,2048]{1,0:T(8,128)(2,1)S(1)}, bf16[128,2048]{1,0:T(8,128)(2,1)}, u32[]{:S(2)}) copy-start(bf16[128,2048]{1,0:T(8,128)(2,1)} %get-tuple-element.9) | copy-start | bytes 1572868
  64.3 1.2 %copy-start.1 = (bf16[128,2048]{1,0:T(8,128)(2,1)S(1)}, bf16[128,2048]{1,0:T(8,128)(2,1)}, u32[]{:S(2)}) copy-start(bf16[128,2048]{1,0:T(8,128)(2,1)} %get-tuple-element.10) | copy-start | bytes 1572868
  65.5 1.2 %copy-start = (bf16[128,2048]{1,0:T(8,128)(2,1)S(1)}, bf16[128,2048]{1,0:T(8,128)(2,1)}, u32[]{:S(2)}) copy-start(bf16[128,2048]{1,0:T(8,128)(2,1)} %get-tuple-element.11) | copy-start | bytes 1572868

commit v2 on v1

--- a/solution.py
+++ b/solution.py
@@ -11,7 +11,7 @@
 HEAD_DIM = 128
 BLOCK = 64
 HALF = BLOCK // 2
-CHUNKS = 4
+CHUNKS = 8
 
 SIB_FINE = 2 * BLOCK
 OUT_FINE = SIB_FINE + BLOCK
@@ -25,7 +25,11 @@
 CAND = FAR_L2 + BLOCK
 COARSE = BLOCK + HALF
 BACK = BLOCK + COARSE + BLOCK
-FWD = BLOCK + HALF + HALF
+RET = BLOCK + HALF
+RELAY_L1 = BLOCK
+RELAY_L2 = 2 * BLOCK
+RELAY = RELAY_L2 + HALF
+STAGES = 14
 
 masked_score = -1e30
 MESH = pl.DeviceIdType.MESH
@@ -67,15 +71,25 @@
 
 
 def kernel(q_ref, k_ref, v_ref, do_ref, att_ref, gq_ref, gk_ref, gv_ref,
-           kv, grad, bias, back_out, back_in, ret_out, ret_in, last_in, send_sem, recv_sem):
+           kv, grad, bias, relay, back_out, back_in, z_out, z_in, s_out, s_in,
+           ret_out, ret_in, send_sem, recv_sem):
     count = lax.axis_size("seq")
     me = lax.axis_index("seq")
     side = lax.rem(me, 2)
+    chip = me // 2
+    odd = lax.rem(chip, 2)
     sib = me + 1 - 2 * side
-    outer = me - 1 + 2 * side
-    has_outer = (outer >= 0) & (outer < count)
-    sib_outer = sib + 1 - 2 * side
-    has_far = (sib_outer >= 0) & (sib_outer < count)
+    is_p = lax.rem(side + chip, 2) == 1
+    is_d = jnp.logical_not(is_p)
+    peer = 2 * (chip + 1 - 2 * odd) + 1 - side
+    step = 4 - 8 * odd
+    has_next = (me + step >= 0) & (me + step < count)
+    has_prev = (me - step >= 0) & (me - step < count)
+    has_outer = is_p | has_prev
+    has_far = is_d | has_prev
+    d_next = is_d & has_next
+    d_prev = is_d & has_prev
+    p_next = is_p & has_next
     feat = q_ref.shape[1]
     width = feat // CHUNKS
     scale = HEAD_DIM ** -0.5
@@ -84,11 +98,25 @@
     inner_half = pl.multiple_of(HALF * (1 - side), HALF)
 
     barrier = pltpu.get_barrier_semaphore()
-    pl.semaphore_signal(barrier, inc=1, device_id={"seq": sib}, device_id_type=MESH)
-
-    @pl.when(has_outer)
+
+    def greet(target):
+        pl.semaphore_signal(barrier, inc=1, device_id={"seq": target}, device_id_type=MESH)
+
+    greet(sib)
+    greet(peer)
+
+    @pl.when(d_next)
     def _():
-        pl.semaphore_signal(barrier, inc=1, device_id={"seq": outer}, device_id_type=MESH)
+        greet(me + step)
+
+    @pl.when(p_next)
+    def _():
+        greet(sib + step)
+
+    @pl.when(d_prev)
+    def _():
+        greet(me - step)
+        greet(sib - step)
 
     own = pl.ds(0, 2 * BLOCK)
     for which, ref in enumerate((k_ref, v_ref)):
@@ -102,6 +130,10 @@
         for which in range(2):
             kv[which, OUT_FINE:OUT_FINE + BLOCK, :] = jnp.zeros((BLOCK, feat), jnp.bfloat16)
             kv[which, OUT_L1:OUT_L1 + 2 * BLOCK, :] = jnp.zeros((2 * BLOCK, feat), jnp.bfloat16)
+
+    @pl.when(is_d & jnp.logical_not(has_next))
+    def _():
+        z_in[:, 0:RET, :] = jnp.zeros((2, RET, feat), jnp.bfloat16)
 
     lane = lax.broadcasted_iota(jnp.int32, (BLOCK, 2 * BLOCK), 1)
     is_outer_lane = (lane >> 6) == side
@@ -118,21 +150,14 @@
     bias[OUT_L2:OUT_L2 + BLOCK] = jnp.where(has_outer, zero + 2.0, masked_score)
     bias[FAR_L2:FAR_L2 + BLOCK] = jnp.where(has_far, zero + 2.0, masked_score)
 
-    @pl.when(has_outer)
-    def _():
-        pl.semaphore_wait(barrier, 2)
-
-    @pl.when(jnp.logical_not(has_outer))
-    def _():
-        pl.semaphore_wait(barrier, 1)
-
-    def part(ref, row, rows, chunk):
-        return ref.at[:, pl.ds(row, rows), pl.ds(chunk * width, width)]
+    peers = 2 + has_next.astype(jnp.int32) + 2 * d_prev.astype(jnp.int32)
+    pl.semaphore_wait(barrier, peers)
 
     def copy(stage, chunk, src, src_row, dst, dst_row, rows, target):
+        cols = pl.ds(chunk * width, width)
         return pltpu.make_async_remote_copy(
-            src_ref=part(src, src_row, rows, chunk),
-            dst_ref=part(dst, dst_row, rows, chunk),
+            src_ref=src.at[:, pl.ds(src_row, rows), cols],
+            dst_ref=dst.at[:, pl.ds(dst_row, rows), cols],
             send_sem=send_sem.at[stage, chunk],
             recv_sem=recv_sem.at[stage, chunk],
             device_id={"seq": target},
@@ -145,54 +170,109 @@
     def sib_coarse(g):
         return copy(1, g, kv, OWN_L1, kv, SIB_L1, COARSE, sib)
 
-    def out_fine(g):
-        return copy(2, g, kv, outer_start, kv, OUT_FINE, BLOCK, outer)
-
-    def out_l1(g):
-        return copy(3, g, kv, OWN_L1 + inner_half, kv, OUT_L1 + HALF, HALF, outer)
-
-    def out_l2(g):
-        return copy(4, g, kv, SIB_L2, kv, OUT_L2 + HALF, HALF, outer)
+    def p_fine(g):
+        return copy(2, g, kv, outer_start, kv, OUT_FINE, BLOCK, peer)
+
+    def p_l1(g):
+        return copy(3, g, kv, OWN_L1 + inner_half, kv, OUT_L1 + HALF, HALF, peer)
+
+    def d_fine(g):
+        return copy(2, g, kv, outer_start, relay, 0, BLOCK, peer)
+
+    def d_l1(g):
+        return copy(3, g, kv, OWN_L1 + inner_half, relay, RELAY_L1 + HALF, HALF, peer)
+
+    def z_fine(g):
+        return copy(4, g, relay, 0, kv, OUT_FINE, BLOCK, me + step)
+
+    def z_l1(g):
+        return copy(5, g, relay, RELAY_L1 + HALF, kv, OUT_L1 + HALF, HALF, me + step)
+
+    def z_l2(g):
+        return copy(6, g, kv, OUT_L2, kv, OUT_L2 + HALF, HALF, sib + step)
+
+    def sib_l2(g):
+        return copy(7, g, relay, RELAY_L2, kv, OUT_L2 + HALF, HALF, sib)
 
     def far(g):
-        return copy(5, g, kv, OUT_L2, kv, FAR_L2, BLOCK, sib)
+        return copy(8, g, kv, OUT_L2, kv, FAR_L2, BLOCK, sib)
 
     def back(g):
-        return copy(6, g, back_out, 0, back_in, 0, BACK, sib)
+        return copy(9, g, back_out, 0, back_in, 0, BACK, sib)
+
+    def z_main(g):
+        return copy(10, g, z_out, 0, z_in, 0, RET, me - step)
+
+    def z_grad2(g):
+        return copy(11, g, z_out, RET, z_in, RET, HALF, sib - step)
+
+    def sib_grad2(g):
+        return copy(12, g, s_out, 0, s_in, 0, HALF, sib)
 
     def ret(g):
-        return copy(7, g, ret_out, 0, ret_in, 0, FWD, outer)
-
-    def last(g):
-        return copy(8, g, ret_in, BLOCK + HALF, last_in, 0, HALF, sib)
+        return copy(13, g, ret_out, 0, ret_in, 0, RET, peer)
 
     for g in range(CHUNKS):
+        @pl.when(is_p)
+        def _():
+            p_fine(g).start()
+            p_l1(g).start()
+
+        @pl.when(is_d)
+        def _():
+            d_fine(g).start()
+            d_l1(g).start()
         sib_coarse(g).start()
         sib_fine(g).start()
-    for g in range(CHUNKS):
-        @pl.when(has_outer)
-        def _():
-            out_fine(g).start()
-            out_l1(g).start()
-        sib_coarse(g).wait_recv()
-
-        @pl.when(has_outer)
-        def _():
-            out_l2(g).start()
-
-    def relay_far(g):
-        cols = pl.ds(g * width, width)
-
-        @pl.when(has_outer)
-        def _():
-            out_fine(g).wait_recv()
-            out_l1(g).wait_recv()
-            out_l2(g).wait_recv()
-            for which in range(2):
-                first = pooled(kv[which, pl.ds(OUT_FINE, BLOCK), cols])
-                kv[which, pl.ds(OUT_L1, HALF), cols] = first
-                second = pooled(kv[which, pl.ds(OUT_L1, BLOCK), cols])
-                kv[which, pl.ds(OUT_L2, HALF), cols] = second
+
+    def derive(ref, which, cols, fine, first, second):
+        ref[which, pl.ds(first, HALF), cols] = pooled(ref[which, pl.ds(fine, BLOCK), cols])
+        ref[which, pl.ds(second, HALF), cols] = pooled(ref[which, pl.ds(first, BLOCK), cols])
+
+    def forward(g):
+        cols = pl.ds(g * width, width)
+
+        @pl.when(is_p)
+        def _():
+            p_fine(g).wait_recv()
+            p_l1(g).wait_recv()
+            for which in range(2):
+                derive(kv, which, cols, OUT_FINE, OUT_L1, OUT_L2)
+
+        @pl.when(p_next)
+        def _():
+            z_l2(g).start()
+
+        @pl.when(is_d)
+        def _():
+            d_fine(g).wait_recv()
+            d_l1(g).wait_recv()
+
+        @pl.when(d_next)
+        def _():
+            z_fine(g).start()
+            z_l1(g).start()
+
+        @pl.when(is_d)
+        def _():
+            for which in range(2):
+                derive(relay, which, cols, 0, RELAY_L1, RELAY_L2)
+            sib_l2(g).start()
+
+    def share_far(g):
+        cols = pl.ds(g * width, width)
+
+        @pl.when(is_p)
+        def _():
+            sib_l2(g).wait_recv()
+
+        @pl.when(d_prev)
+        def _():
+            z_fine(g).wait_recv()
+            z_l1(g).wait_recv()
+            for which in range(2):
+                derive(kv, which, cols, OUT_FINE, OUT_L1, OUT_L2)
+            z_l2(g).wait_recv()
         far(g).start()
 
     def attend(h):
@@ -234,69 +314,119 @@
             grad[which, rows, cols] += take(0, BLOCK)
             rows = pl.ds(OWN_L1, COARSE)
             grad[which, rows, cols] += take(BLOCK, COARSE)
-
-        @pl.when(has_outer)
-        def _():
-            for which in range(2):
-                second = (grad[which, pl.ds(OUT_L2, BLOCK), cols]
-                          + back_in[which, pl.ds(BLOCK + COARSE, BLOCK), cols].astype(jnp.float32))
+            rows = pl.ds(OUT_L2, BLOCK)
+            grad[which, rows, cols] += take(BLOCK + COARSE, BLOCK)
+
+        @pl.when(d_prev)
+        def _():
+            for which in range(2):
+                second = grad[which, pl.ds(OUT_L2, BLOCK), cols]
                 first = grad[which, pl.ds(OUT_L1, BLOCK), cols] + spread(second[:HALF])
+                fine = grad[which, pl.ds(OUT_FINE, BLOCK), cols] + spread(first[:HALF])
+                z_out[which, pl.ds(0, BLOCK), cols] = fine.astype(jnp.bfloat16)
+                z_out[which, pl.ds(BLOCK, HALF), cols] = first[HALF:].astype(jnp.bfloat16)
+                z_out[which, pl.ds(RET, HALF), cols] = second[HALF:].astype(jnp.bfloat16)
+            z_main(g).start()
+            z_grad2(g).start()
+
+        @pl.when(is_p)
+        def _():
+            for which in range(2):
+                s_out[which, :, cols] = grad[which, pl.ds(OUT_L2 + HALF, HALF), cols].astype(jnp.bfloat16)
+            sib_grad2(g).start()
+
+    def send_peer(g):
+        cols = pl.ds(g * width, width)
+
+        @pl.when(p_next)
+        def _():
+            z_grad2(g).wait_recv()
+            for which in range(2):
+                grad[which, pl.ds(OUT_L2, HALF), cols] += (
+                    z_in[which, pl.ds(RET, HALF), cols].astype(jnp.float32))
+
+        @pl.when(is_p)
+        def _():
+            for which in range(2):
+                first = (grad[which, pl.ds(OUT_L1, BLOCK), cols]
+                         + spread(grad[which, pl.ds(OUT_L2, HALF), cols]))
                 fine = grad[which, pl.ds(OUT_FINE, BLOCK), cols] + spread(first[:HALF])
                 ret_out[which, pl.ds(0, BLOCK), cols] = fine.astype(jnp.bfloat16)
                 ret_out[which, pl.ds(BLOCK, HALF), cols] = first[HALF:].astype(jnp.bfloat16)
-                ret_out[which, pl.ds(BLOCK + HALF, HALF), cols] = second[HALF:].astype(jnp.bfloat16)
-            ret(g).start()
-
-    def take_outer(g):
-        cols = pl.ds(g * width, width)
-
-        @pl.when(has_outer)
-        def _():
-            ret(g).wait_recv()
-            last(g).start()
-            for which in range(2):
-                rows = pl.ds(outer_start, BLOCK)
-                grad[which, rows, cols] += ret_in[which, pl.ds(0, BLOCK), cols].astype(jnp.float32)
-                rows = pl.ds(OWN_L1 + inner_half, HALF)
-                grad[which, rows, cols] += ret_in[which, pl.ds(BLOCK, HALF), cols].astype(jnp.float32)
+
+        @pl.when(d_next)
+        def _():
+            z_main(g).wait_recv()
+
+        @pl.when(is_d)
+        def _():
+            sib_grad2(g).wait_recv()
+            for which in range(2):
+                first = spread(s_in[which, :, cols].astype(jnp.float32))
+                fine = spread(first[:HALF])
+                fine += z_in[which, pl.ds(0, BLOCK), cols].astype(jnp.float32)
+                rest = first[HALF:] + z_in[which, pl.ds(BLOCK, HALF), cols].astype(jnp.float32)
+                ret_out[which, pl.ds(0, BLOCK), cols] = fine.astype(jnp.bfloat16)
+                ret_out[which, pl.ds(BLOCK, HALF), cols] = rest.astype(jnp.bfloat16)
+        ret(g).start()
 
     def finish(g):
         cols = pl.ds(g * width, width)
-
-        @pl.when(has_far)
-        def _():
-            last(g).wait_recv()
-            for which in range(2):
-                rows = pl.ds(OWN_L2, HALF)
-                grad[which, rows, cols] += last_in[which, :, cols].astype(jnp.float32)
+        ret(g).wait_recv()
         for which, ref in enumerate((gk_ref, gv_ref)):
+            rows = pl.ds(outer_start, BLOCK)
+            grad[which, rows, cols] += ret_in[which, pl.ds(0, BLOCK), cols].astype(jnp.float32)
+            rows = pl.ds(OWN_L1 + inner_half, HALF)
+            grad[which, rows, cols] += ret_in[which, pl.ds(BLOCK, HALF), cols].astype(jnp.float32)
             first = grad[which, pl.ds(OWN_L1, BLOCK), cols] + spread(grad[which, pl.ds(OWN_L2, HALF), cols])
             fine = grad[which, pl.ds(0, 2 * BLOCK), cols] + spread(first)
             ref[:, cols] = fine.astype(jnp.bfloat16)
 
     heads = width // HEAD_DIM
+    forward(0)
     for g in range(CHUNKS):
-        relay_far(g)
+        if g + 1 < CHUNKS:
+            forward(g + 1)
+        share_far(g)
+        sib_coarse(g).wait_recv()
         sib_fine(g).wait_recv()
         far(g).wait_recv()
         lax.fori_loop(g * heads, (g + 1) * heads, lambda h, c: (attend(h), c)[1], 0)
         send_back(g)
         if g > 0:
             send_outer(g - 1)
+        if g > 1:
+            send_peer(g - 2)
     send_outer(CHUNKS - 1)
+    for g in range(max(0, CHUNKS - 2), CHUNKS):
+        send_peer(g)
     for g in range(CHUNKS):
-        take_outer(g)
-        if g > 0:
-            finish(g - 1)
-    finish(CHUNKS - 1)
+        finish(g)
     for g in range(CHUNKS):
-        for item in (sib_fine, sib_coarse, far, back):
+        for item in (sib_fine, sib_coarse, p_fine, p_l1, far, back, ret):
             item(g).wait_send()
 
-        @pl.when(has_outer)
-        def _():
-            for item in (out_fine, out_l1, out_l2, ret, last):
-                item(g).wait_send()
+        @pl.when(is_p)
+        def _():
+            sib_grad2(g).wait_send()
+
+        @pl.when(is_d)
+        def _():
+            sib_l2(g).wait_send()
+
+        @pl.when(p_next)
+        def _():
+            z_l2(g).wait_send()
+
+        @pl.when(d_next)
+        def _():
+            z_fine(g).wait_send()
+            z_l1(g).wait_send()
+
+        @pl.when(d_prev)
+        def _():
+            z_main(g).wait_send()
+            z_grad2(g).wait_send()
 
 
 def body(queries, key_input, value_input, cotangent):
@@ -312,13 +442,17 @@
             pltpu.VMEM((2, CAND, feat), jnp.bfloat16),
             pltpu.VMEM((2, CAND, feat), jnp.float32),
             pltpu.VMEM((CAND, rows), jnp.float32),
+            pltpu.VMEM((2, RELAY, feat), jnp.bfloat16),
             pltpu.VMEM((2, BACK, feat), jnp.bfloat16),
             pltpu.VMEM((2, BACK, feat), jnp.bfloat16),
-            pltpu.VMEM((2, FWD, feat), jnp.bfloat16),
-            pltpu.VMEM((2, FWD, feat), jnp.bfloat16),
+            pltpu.VMEM((2, RET + HALF, feat), jnp.bfloat16),
+            pltpu.VMEM((2, RET + HALF, feat), jnp.bfloat16),
             pltpu.VMEM((2, HALF, feat), jnp.bfloat16),
-            pltpu.SemaphoreType.DMA((9, CHUNKS)),
-            pltpu.SemaphoreType.DMA((9, CHUNKS)),
+            pltpu.VMEM((2, HALF, feat), jnp.bfloat16),
+            pltpu.VMEM((2, RET, feat), jnp.bfloat16),
+            pltpu.VMEM((2, RET, feat), jnp.bfloat16),
+            pltpu.SemaphoreType.DMA((STAGES, CHUNKS)),
+            pltpu.SemaphoreType.DMA((STAGES, CHUNKS)),
         ],
         compiler_params=pltpu.CompilerParams(
             collective_id=0, has_side_effects=True, vmem_limit_bytes=56 * 1024 * 1024),

time: 67.8 us -> 64.1 us (0.945)
  Pallas kernels: 61.7 us -> 57.6 us
    pallas_call x1, Pallas kernels: 61.7 us -> 57.6 us  [body(): pl.pallas_call(kernel, name='hier_attention', out_shape=[out] * 4, in_spe...]
where the time goes in v2:
time: 64.1 us; the launch traced here: 63.5 us
  Pallas kernels  57.6 us (90%)
  local copies, waits for them, and re-layouts  5.19 us (8%)
  between operations  0.65 us (1%)
    pallas_call x1, Pallas kernels, body(): pl.pallas_call(kernel, name='hier_attention', out_shape=[out] * 4, in_spe...  57.6 us
    unnamed x10, local copies, waits for them, and re-layouts  5.19 us

profile of v2, /device:TPU:21, one launch (start us, length us, event | category | flops | bytes accessed | tf_op | source)
XLA Modules:
  0.0 63.5 jit_solution(14143996345679827836)
XLA Ops:
  0.6 57.6 %hier_attention.1 = (bf16[128,2048]{1,0:T(8,128)(2,1)}, bf16[128,2048]{1,0:T(8,128)(2,1)}, bf16[128,2048]{1,0:T(8,128)(2,1)}, bf16[128,2048]{1,0:T(8,128)(2,1)}) custom-call(bf16[128,2048]{1,0:T(8,128)(2,1)} %q_ref.1, bf16[128,2048]{1,0:T(8,128)(2,1)} %k_ref.1, bf16[128,2048]{1,0:T(8,128)(2,1)} %v_ref.1, bf16[128,2048]{1,0:T(8,128)(2,1)} %do_ref.1), custom_call_target="tpu_custom_call" | custom-call | tf_op jit(solution)/shard_map/hier_attention/pallas_call | solution.py:435
  58.3 0.0 copy-start.2
  58.3 1.9 %copy.12 = bf16[128,2048]{1,0:T(8,128)(2,1)} copy(bf16[128,2048]{1,0:T(8,128)(2,1)} %get-tuple-element.8) | data formatting | bytes 1048576
  60.2 0.0 copy-done.2
  60.2 0.0 copy-start.1
  60.2 0.8 %copy.13 = bf16[128,2048]{1,0:T(8,128)(2,1)} copy(bf16[128,2048]{1,0:T(8,128)(2,1)S(1)} %copy-done.2) | data formatting | bytes 1048576
  61.0 0.4 copy-done.1
  61.5 0.0 copy-start
  61.5 0.8 %copy.14 = bf16[128,2048]{1,0:T(8,128)(2,1)} copy(bf16[128,2048]{1,0:T(8,128)(2,1)S(1)} %copy-done.1) | data formatting | bytes 1048576
  62.3 0.4 copy-done
  62.7 0.8 %copy.15 = bf16[128,2048]{1,0:T(8,128)(2,1)} copy(bf16[128,2048]{1,0:T(8,128)(2,1)S(1)} %copy-done) | data formatting | bytes 1048576
Async XLA Ops:
  58.3 2.0 %copy-start.2 = (bf16[128,2048]{1,0:T(8,128)(2,1)S(1)}, bf16[128,2048]{1,0:T(8,128)(2,1)}, u32[]{:S(2)}) copy-start(bf16[128,2048]{1,0:T(8,128)(2,1)} %get-tuple-element.9) | copy-start | bytes 1572868
  60.2 1.2 %copy-start.1 = (bf16[128,2048]{1,0:T(8,128)(2,1)S(1)}, bf16[128,2048]{1,0:T(8,128)(2,1)}, u32[]{:S(2)}) copy-start(bf16[128,2048]{1,0:T(8,128)(2,1)} %get-tuple-element.10) | copy-start | bytes 1572868
  61.5 1.2 %copy-start = (bf16[128,2048]{1,0:T(8,128)(2,1)S(1)}, bf16[128,2048]{1,0:T(8,128)(2,1)}, u32[]{:S(2)}) copy-start(bf16[128,2048]{1,0:T(8,128)(2,1)} %get-tuple-element.11) | copy-start | bytes 1572868

commit v3 on v2

--- a/solution.py
+++ b/solution.py
@@ -12,6 +12,8 @@
 BLOCK = 64
 HALF = BLOCK // 2
 CHUNKS = 8
+EARLY = 2
+LAG = 8
 
 SIB_FINE = 2 * BLOCK
 OUT_FINE = SIB_FINE + BLOCK
@@ -53,21 +55,41 @@
     return jnp.where((col >> 1) == row, 0.5, 0.0).astype(jnp.bfloat16)
 
 
-def spread_matrix(rows):
-    row = lax.broadcasted_iota(jnp.int32, (2 * rows, rows), 0)
-    col = lax.broadcasted_iota(jnp.int32, (2 * rows, rows), 1)
-    return jnp.where((row >> 1) == col, 0.5, 0.0).astype(jnp.bfloat16)
-
-
 def pooled(rows):
     return nn(pool_matrix(rows.shape[0]), rows).astype(jnp.bfloat16)
 
 
-def spread(grads):
-    matrix = spread_matrix(grads.shape[0])
+def spread_matrix(shape, row0, col0, rows, shift):
+    row = lax.broadcasted_iota(jnp.int32, shape, 0) - row0
+    col = lax.broadcasted_iota(jnp.int32, shape, 1) - col0
+    hit = (row >= 0) & (row < rows) & ((row >> shift) == col)
+    return jnp.where(hit, 0.5 ** shift, 0.0)
+
+
+def spread(matrix, grads):
+    matrix = matrix.astype(jnp.bfloat16)
     high = grads.astype(jnp.bfloat16)
     low = (grads - high.astype(jnp.float32)).astype(jnp.bfloat16)
-    return nn(matrix, high) + nn(matrix, low)
+    return nn(jnp.concatenate([matrix, matrix], axis=1), jnp.concatenate([high, low], axis=0))
+
+
+def message_matrix():
+    shape = (RET, BLOCK)
+    return (spread_matrix(shape, 0, 0, BLOCK, 1)
+            + spread_matrix(shape, 0, HALF, BLOCK, 2)
+            + spread_matrix(shape, BLOCK, HALF + HALF // 2, HALF, 1))
+
+
+def coarse_matrix():
+    shape = (RET, HALF)
+    return (spread_matrix(shape, 0, 0, BLOCK, 2)
+            + spread_matrix(shape, BLOCK, HALF // 2, HALF, 1)).astype(jnp.bfloat16)
+
+
+def own_matrix():
+    shape = (2 * BLOCK, COARSE)
+    return (spread_matrix(shape, 0, 0, 2 * BLOCK, 1)
+            + spread_matrix(shape, 0, BLOCK, 2 * BLOCK, 2))
 
 
 def kernel(q_ref, k_ref, v_ref, do_ref, att_ref, gq_ref, gk_ref, gv_ref,
@@ -121,9 +143,6 @@
     own = pl.ds(0, 2 * BLOCK)
     for which, ref in enumerate((k_ref, v_ref)):
         kv[which, own, :] = ref[...]
-        first = pooled(ref[...])
-        kv[which, OWN_L1:OWN_L1 + BLOCK, :] = first
-        kv[which, OWN_L2:OWN_L2 + HALF, :] = pooled(first)
 
     @pl.when(jnp.logical_not(has_outer))
     def _():
@@ -212,16 +231,34 @@
     def ret(g):
         return copy(13, g, ret_out, 0, ret_in, 0, RET, peer)
 
+    def start_fine(g):
+        @pl.when(is_p)
+        def _():
+            p_fine(g).start()
+
+        @pl.when(is_d)
+        def _():
+            d_fine(g).start()
+
+    def start_l1(g):
+        @pl.when(is_p)
+        def _():
+            p_l1(g).start()
+
+        @pl.when(is_d)
+        def _():
+            d_l1(g).start()
+
+    for g in range(EARLY):
+        start_fine(g)
+    for which in range(2):
+        first = pooled(kv[which, own, :])
+        kv[which, OWN_L1:OWN_L1 + BLOCK, :] = first
+        kv[which, OWN_L2:OWN_L2 + HALF, :] = pooled(first)
     for g in range(CHUNKS):
-        @pl.when(is_p)
-        def _():
-            p_fine(g).start()
-            p_l1(g).start()
-
-        @pl.when(is_d)
-        def _():
-            d_fine(g).start()
-            d_l1(g).start()
+        if g >= EARLY:
+            start_fine(g)
+        start_l1(g)
         sib_coarse(g).start()
         sib_fine(g).start()
 
@@ -292,17 +329,20 @@
         row_dots = jnp.sum(product.T, axis=0, keepdims=True)
         grad_scores = (weights * (nt(v, do) - row_dots) * scale).astype(jnp.bfloat16)
         gq_ref[:, cols] = tn(grad_scores, k).astype(jnp.bfloat16)
-        grad[0, :, cols] = nn(grad_scores, q)
-        grad[1, :, cols] = nn(weights_b, do)
-
-    def send_back(g):
-        cols = pl.ds(g * width, width)
-        for which in range(2):
+        for which, part in ((0, nn(grad_scores, q)), (1, nn(weights_b, do))):
+            for start, end in ((0, SIB_FINE), (OUT_FINE, SIB_L1), (OUT_L1, FAR_L2)):
+                grad[which, start:end, cols] = part[start:end]
             for dst, src, rows in ((0, SIB_FINE, BLOCK), (BLOCK, SIB_L1, COARSE),
                                    (BLOCK + COARSE, FAR_L2, BLOCK)):
-                back_out[which, pl.ds(dst, rows), cols] = (
-                    grad[which, pl.ds(src, rows), cols].astype(jnp.bfloat16))
-        back(g).start()
+                back_out[which, dst:dst + rows, cols] = part[src:src + rows].astype(jnp.bfloat16)
+
+    def folded(which, cols):
+        coarse = jnp.concatenate([grad[which, pl.ds(OUT_L1, HALF), cols],
+                                  grad[which, pl.ds(OUT_L2, HALF), cols]], axis=0)
+        total = spread(message_matrix(), coarse)
+        total += jnp.concatenate([grad[which, pl.ds(OUT_FINE, BLOCK), cols],
+                                  grad[which, pl.ds(OUT_L1 + HALF, HALF), cols]], axis=0)
+        return total.astype(jnp.bfloat16)
 
     def send_outer(g):
         cols = pl.ds(g * width, width)
@@ -320,12 +360,9 @@
         @pl.when(d_prev)
         def _():
             for which in range(2):
-                second = grad[which, pl.ds(OUT_L2, BLOCK), cols]
-                first = grad[which, pl.ds(OUT_L1, BLOCK), cols] + spread(second[:HALF])
-                fine = grad[which, pl.ds(OUT_FINE, BLOCK), cols] + spread(first[:HALF])
-                z_out[which, pl.ds(0, BLOCK), cols] = fine.astype(jnp.bfloat16)
-                z_out[which, pl.ds(BLOCK, HALF), cols] = first[HALF:].astype(jnp.bfloat16)
-                z_out[which, pl.ds(RET, HALF), cols] = second[HALF:].astype(jnp.bfloat16)
+                z_out[which, pl.ds(0, RET), cols] = folded(which, cols)
+                second = grad[which, pl.ds(OUT_L2 + HALF, HALF), cols]
+                z_out[which, pl.ds(RET, HALF), cols] = second.astype(jnp.bfloat16)
             z_main(g).start()
             z_grad2(g).start()
 
@@ -348,11 +385,7 @@
         @pl.when(is_p)
         def _():
             for which in range(2):
-                first = (grad[which, pl.ds(OUT_L1, BLOCK), cols]
-                         + spread(grad[which, pl.ds(OUT_L2, HALF), cols]))
-                fine = grad[which, pl.ds(OUT_FINE, BLOCK), cols] + spread(first[:HALF])
-                ret_out[which, pl.ds(0, BLOCK), cols] = fine.astype(jnp.bfloat16)
-                ret_out[which, pl.ds(BLOCK, HALF), cols] = first[HALF:].astype(jnp.bfloat16)
+                ret_out[which, :, cols] = folded(which, cols)
 
         @pl.when(d_next)
         def _():
@@ -362,12 +395,9 @@
         def _():
             sib_grad2(g).wait_recv()
             for which in range(2):
-                first = spread(s_in[which, :, cols].astype(jnp.float32))
-                fine = spread(first[:HALF])
-                fine += z_in[which, pl.ds(0, BLOCK), cols].astype(jnp.float32)
-                rest = first[HALF:] + z_in[which, pl.ds(BLOCK, HALF), cols].astype(jnp.float32)
-                ret_out[which, pl.ds(0, BLOCK), cols] = fine.astype(jnp.bfloat16)
-                ret_out[which, pl.ds(BLOCK, HALF), cols] = rest.astype(jnp.bfloat16)
+                total = nn(coarse_matrix(), s_in[which, :, cols])
+                total += z_in[which, pl.ds(0, RET), cols].astype(jnp.float32)
+                ret_out[which, :, cols] = total.astype(jnp.bfloat16)
         ret(g).start()
 
     def finish(g):
@@ -378,8 +408,8 @@
             grad[which, rows, cols] += ret_in[which, pl.ds(0, BLOCK), cols].astype(jnp.float32)
             rows = pl.ds(OWN_L1 + inner_half, HALF)
             grad[which, rows, cols] += ret_in[which, pl.ds(BLOCK, HALF), cols].astype(jnp.float32)
-            first = grad[which, pl.ds(OWN_L1, BLOCK), cols] + spread(grad[which, pl.ds(OWN_L2, HALF), cols])
-            fine = grad[which, pl.ds(0, 2 * BLOCK), cols] + spread(first)
+            fine = grad[which, pl.ds(0, 2 * BLOCK), cols]
+            fine += spread(own_matrix(), grad[which, pl.ds(OWN_L1, COARSE), cols])
             ref[:, cols] = fine.astype(jnp.bfloat16)
 
     heads = width // HEAD_DIM
@@ -391,16 +421,18 @@
         sib_coarse(g).wait_recv()
         sib_fine(g).wait_recv()
         far(g).wait_recv()
-        lax.fori_loop(g * heads, (g + 1) * heads, lambda h, c: (attend(h), c)[1], 0)
-        send_back(g)
+        lax.fori_loop(g * heads, (g + 1) * heads, lambda h, c: (attend(h), c)[1], 0, unroll=2)
+        back(g).start()
         if g > 0:
             send_outer(g - 1)
         if g > 1:
             send_peer(g - 2)
+        if g >= LAG:
+            finish(g - LAG)
     send_outer(CHUNKS - 1)
     for g in range(max(0, CHUNKS - 2), CHUNKS):
         send_peer(g)
-    for g in range(CHUNKS):
+    for g in range(max(0, CHUNKS - LAG), CHUNKS):
         finish(g)
     for g in range(CHUNKS):
         for item in (sib_fine, sib_coarse, p_fine, p_l1, far, back, ret):
@@ -429,10 +461,19 @@
             z_grad2(g).wait_send()
 
 
+def place(*refs):
+    sems = refs[-1]
+    copies = [pltpu.make_async_copy(refs[i], refs[4 + i], sems.at[i]) for i in range(4)]
+    for item in copies:
+        item.start()
+    for item in copies:
+        item.wait()
+
+
 def body(queries, key_input, value_input, cotangent):
     rows, feat = queries.shape
     out = jax.ShapeDtypeStruct((rows, feat), jnp.bfloat16)
-    return tuple(pl.pallas_call(
+    results = pl.pallas_call(
         kernel,
         name="hier_attention",
         out_shape=[out] * 4,
@@ -456,7 +497,15 @@
         ],
         compiler_params=pltpu.CompilerParams(
             collective_id=0, has_side_effects=True, vmem_limit_bytes=56 * 1024 * 1024),
-    )(queries, key_input, value_input, cotangent))
+    )(queries, key_input, value_input, cotangent)
+    return tuple(pl.pallas_call(
+        place,
+        name="place",
+        out_shape=[out] * 4,
+        in_specs=[pl.BlockSpec(memory_space=pltpu.VMEM)] * 4,
+        out_specs=[pl.BlockSpec(memory_space=pl.ANY)] * 4,
+        scratch_shapes=[pltpu.SemaphoreType.DMA((4,))],
+    )(*results))
 
 
 def solution(mesh):

time: 64.1 us -> 61 us (0.952)
  local copies, waits for them, and re-layouts: 5.19 us -> 0 us
  Pallas kernels: 57.6 us -> 59.1 us
    unnamed x10 -> x0, local copies, waits for them, and re-layouts: 5.19 us -> none
    pallas_call x0 -> x1, Pallas kernels: none -> 2.86 us  [body(): pl.pallas_call(place, name='place', out_shape=[out] * 4, in_specs=[pl.Blo...]
    pallas_call x1, Pallas kernels: 57.6 us -> 56.2 us  [body(): pl.pallas_call(kernel, name='hier_attention', out_shape=[out] * 4, in_spe...]
where the time goes in v3:
time: 61 us; the launch traced here: 59.9 us
  Pallas kernels  59.1 us (97%)
  between operations  0.8 us (1%)
    pallas_call x1, Pallas kernels, body(): pl.pallas_call(kernel, name='hier_attention', out_shape=[out] * 4, in_spe...  56.2 us
    pallas_call x1, Pallas kernels, body(): pl.pallas_call(place, name='place', out_shape=[out] * 4, in_specs=[pl.Blo...  2.86 us

profile of v3, /device:TPU:21, one launch (start us, length us, event | category | flops | bytes accessed | tf_op | source)
XLA Modules:
  0.0 59.9 jit_solution(12043708853363210923)
XLA Ops:
  0.6 56.2 %hier_attention.1 = (bf16[128,2048]{1,0:T(8,128)(2,1)}, bf16[128,2048]{1,0:T(8,128)(2,1)}, bf16[128,2048]{1,0:T(8,128)(2,1)}, bf16[128,2048]{1,0:T(8,128)(2,1)}) custom-call(bf16[128,2048]{1,0:T(8,128)(2,1)} %q_ref.1, bf16[128,2048]{1,0:T(8,128)(2,1)} %k_ref.1, bf16[128,2048]{1,0:T(8,128)(2,1)} %v_ref.1, bf16[128,2048]{1,0:T(8,128)(2,1)} %do_ref.1), custom_call_target="tpu_custom_call" | custom-call | tf_op jit(solution)/shard_map/hier_attention/pallas_call | solution.py:476
  56.8 2.9 %place.1 = (bf16[128,2048]{1,0:T(8,128)(2,1)}, bf16[128,2048]{1,0:T(8,128)(2,1)}, bf16[128,2048]{1,0:T(8,128)(2,1)}, bf16[128,2048]{1,0:T(8,128)(2,1)}) custom-call(bf16[128,2048]{1,0:T(8,128)(2,1)} %get-tuple-element.8.refs_0_, bf16[128,2048]{1,0:T(8,128)(2,1)} %get-tuple-element.9.refs_1_, bf16[128,2048]{1,0:T(8,128)(2,1)} %get-tuple-element.10.refs_2_, ...), custom_call_target="tpu_custom_call" | custom-call | tf_op jit(solution)/shard_map/place/pallas_call | solution.py:501

commit v4 on v3

--- a/solution.py
+++ b/solution.py
@@ -462,11 +462,15 @@
 
 
 def place(*refs):
-    sems = refs[-1]
-    copies = [pltpu.make_async_copy(refs[i], refs[4 + i], sems.at[i]) for i in range(4)]
-    for item in copies:
+    held, sems = refs[8:]
+    loads = [pltpu.make_async_copy(refs[i], held.at[i], sems.at[0, i]) for i in range(4)]
+    stores = [pltpu.make_async_copy(held.at[i], refs[4 + i], sems.at[1, i]) for i in range(4)]
+    for item in loads:
         item.start()
-    for item in copies:
+    for load, store in zip(loads, stores):
+        load.wait()
+        store.start()
+    for item in stores:
         item.wait()
 
 
@@ -502,9 +506,9 @@
         place,
         name="place",
         out_shape=[out] * 4,
-        in_specs=[pl.BlockSpec(memory_space=pltpu.VMEM)] * 4,
+        in_specs=[pl.BlockSpec(memory_space=pl.ANY)] * 4,
         out_specs=[pl.BlockSpec(memory_space=pl.ANY)] * 4,
-        scratch_shapes=[pltpu.SemaphoreType.DMA((4,))],
+        scratch_shapes=[pltpu.VMEM((4, rows, feat), jnp.bfloat16), pltpu.SemaphoreType.DMA((2, 4))],
     )(*results))
 
 

time: 61 us -> 60.6 us (level)
  no operation moved by 1% of the time
where the time goes in v4:
time: 60.6 us; the launch traced here: 59.4 us
  Pallas kernels  58.6 us (97%)
  between operations  0.8 us (1%)
    pallas_call x1, Pallas kernels, body(): pl.pallas_call(kernel, name='hier_attention', out_shape=[out] * 4, in_spe...  56.2 us
    pallas_call x1, Pallas kernels, body(): pl.pallas_call(place, name='place', out_shape=[out] * 4, in_specs=[pl.Blo...  2.42 us

profile of v4, /device:TPU:21, one launch (start us, length us, event | category | flops | bytes accessed | tf_op | source)
XLA Modules:
  0.0 59.4 jit_solution(1536642614662999643)
XLA Ops:
  0.6 56.2 %hier_attention.1 = (bf16[128,2048]{1,0:T(8,128)(2,1)}, bf16[128,2048]{1,0:T(8,128)(2,1)}, bf16[128,2048]{1,0:T(8,128)(2,1)}, bf16[128,2048]{1,0:T(8,128)(2,1)}) custom-call(bf16[128,2048]{1,0:T(8,128)(2,1)} %q_ref.1, bf16[128,2048]{1,0:T(8,128)(2,1)} %k_ref.1, bf16[128,2048]{1,0:T(8,128)(2,1)} %v_ref.1, bf16[128,2048]{1,0:T(8,128)(2,1)} %do_ref.1), custom_call_target="tpu_custom_call" | custom-call | tf_op jit(solution)/shard_map/hier_attention/pallas_call | solution.py:480
  56.8 2.4 %place.1 = (bf16[128,2048]{1,0:T(8,128)(2,1)}, bf16[128,2048]{1,0:T(8,128)(2,1)}, bf16[128,2048]{1,0:T(8,128)(2,1)}, bf16[128,2048]{1,0:T(8,128)(2,1)}) custom-call(bf16[128,2048]{1,0:T(8,128)(2,1)} %get-tuple-element.8.refs_0_, bf16[128,2048]{1,0:T(8,128)(2,1)} %get-tuple-element.9.refs_1_, bf16[128,2048]{1,0:T(8,128)(2,1)} %get-tuple-element.10.refs_2_, ...), custom_call_target="tpu_custom_call" | custom-call | tf_op jit(solution)/shard_map/place/pallas_call | solution.py:505
